TPU v7x, 32 devices: a whole 2x2x4 slice. The times are simulated.
32 devices in a mesh: row: 4 (over z), col: 8 (over y, x, core).
Axes of the slice: x: 2, y: 2, z: 4, core: 2. Of those that a mesh axis runs over, the one named last changes fastest.
Arguments:
- matrix: float32 [16384, 4096], P('row', 'col'), may hold values from -6 to 6
- leaf_v: float32 [2, 16384, 256], P(None, ('row', 'col')), may hold values from -0.09375 to 0.09375
- leaf_t: float32 [2, 1024, 256], P(None, 'row'), may hold values from -0.375 to 0.375
- tree_v: float32 [2, 3, 512, 256], replicated, may hold values from -0.25 to 0.25
- tree_t: float32 [2, 3, 256, 256], replicated, may hold values from -0.375 to 0.375
Outputs:
- updated: float32 [16384, 4096], P('row', 'col')
All inputs are finite; a program needn't handle non-finite values.
Results may differ from a plain program's by a relative error of at most 0.0001.
Values sent between devices are 32-bit elements; how exact they have to be, the bound alone decides.
A program may use at most 128 MiB of HBM per device.

v0:
```python
import functools

import jax
import jax.numpy as jnp
from jax import lax
from jax.experimental import pallas as pl
from jax.experimental.pallas import tpu as pltpu
from jax.sharding import PartitionSpec as P

MESH = pl.DeviceIdType.MESH


def flip(index, mask):
    bit = 1
    while bit <= mask:
        if mask & bit:
            index = index + bit - 2 * bit * lax.rem(lax.div(index, bit), 2)
        bit *= 2
    return index


def halves(x):
    high = x.astype(jnp.bfloat16)
    return high, (x - high.astype(jnp.float32)).astype(jnp.bfloat16)


def product(left, right, dims):
    def one(a, b):
        return lax.dot_general(a, b, (dims, ((), ())), preferred_element_type=jnp.float32)

    (lh, ll), (rh, rl) = left, right
    return one(lh, rh) + (one(lh, rl) + one(ll, rh))


def left_product(left, right):
    return product(halves(left), halves(right), ((0,), (0,)))


def right_product(left, right):
    return product(halves(left), right, ((1,), (0,)))


def tile_of(rows, step, most):
    count = rows // step
    best = max(k for k in range(1, most // step + 1) if count % k == 0)
    return best * step


def kernel(grid_rows, chips, matrix, leaf_v, leaf_t, tree_v, tree_t, out,
           work, vectors, inner, scaled, top, other, pair_v, pair_t,
           load_sem, tree_sem, store_sem, send_sem, recv_sem, core_send, core_recv, top_send, top_recv):
    panels, own_rows, width = leaf_v.shape
    rows = work.shape[0]
    levels = grid_rows.bit_length() - 1
    bits = chips.bit_length() - 1
    half_rows = own_rows // 2
    unit = 2 * own_rows
    position = lax.axis_index("row")
    column = lax.axis_index("col")
    chip = lax.div(column, 2)
    core = lax.rem(column, 2)

    def device(which_chip, which_core):
        return {"row": position, "col": which_chip * 2 + which_core}

    def load_work(r):
        start = pl.ds(pl.multiple_of(flip(chip, r) * unit, unit), unit)
        return pltpu.make_async_copy(matrix.at[start], work.at[start], load_sem.at[panels + r])

    def load_own(p):
        start = pl.ds(pl.multiple_of(column * own_rows, own_rows), own_rows)
        return pltpu.make_async_copy(leaf_v.at[p], vectors.at[p, start], load_sem.at[p])

    def load_pair(p, level):
        node = grid_rows - (grid_rows >> level) + lax.div(position, 2 << level)
        return (pltpu.make_async_copy(tree_v.at[p, node], pair_v.at[p, level], tree_sem.at[p, level, 0]),
                pltpu.make_async_copy(tree_t.at[p, node], pair_t.at[p, level], tree_sem.at[p, level, 1]))

    load_own(0).start()
    for r in range(chips):
        load_work(r).start()
    for p in range(1, panels):
        load_own(p).start()
    for p in range(panels):
        for level in range(levels):
            for copy in load_pair(p, level):
                copy.start()

    barrier = pltpu.get_barrier_semaphore()
    partners = [device(chip, 1 - core)]
    partners += [device(flip(chip, 1 << b), core) for b in range(bits)]
    partners += [{"row": flip(position, 1 << level), "col": column} for level in range(levels)]
    for partner in partners:
        pl.semaphore_signal(barrier, inc=1, device_id=partner, device_id_type=MESH)
    pl.semaphore_wait(barrier, len(partners))

    orders = [list(range(bits)), list(reversed(range(bits)))]

    def piece(p, r, h, on_core):
        start = (flip(chip, r) * 2 + on_core) * own_rows + h * half_rows
        return vectors.at[p, pl.ds(pl.multiple_of(start, half_rows), half_rows)]

    def source(p, r, h):
        if r == 0:
            return leaf_v.at[p, pl.ds(h * half_rows, half_rows)]
        return piece(p, r, h, core)

    def chip_copy(p, r, h, bit):
        return pltpu.make_async_remote_copy(
            source(p, r, h), piece(p, r, h, core), send_sem.at[p, r, h, bit],
            recv_sem.at[p, r | 1 << bit, h], device_id=device(flip(chip, 1 << bit), core), device_id_type=MESH)

    def core_copy(p, r, h):
        return pltpu.make_async_remote_copy(
            source(p, r, h), piece(p, r, h, core), core_send.at[p, r, h],
            core_recv.at[p, r, h], device_id=device(chip, 1 - core), device_id_type=MESH)

    def core_arrival(p, r, h):
        there = piece(p, r, h, 1 - core)
        pltpu.make_async_remote_copy(
            there, there, core_send.at[p, r, h], core_recv.at[p, r, h],
            device_id=device(chip, 1 - core), device_id_type=MESH).wait_recv()

    def chip_arrival(p, r, h):
        here = piece(p, r, h, core)
        pltpu.make_async_remote_copy(
            here, here, core_send.at[p, r, h], recv_sem.at[p, r, h],
            device_id=device(chip, 1 - core), device_id_type=MESH).wait_recv()

    started = []

    def start(copy):
        copy.start()
        started.append(copy)

    def send_own(p):
        for k in range(bits):
            for h in range(2):
                start(chip_copy(p, 0, h, orders[h][k]))
        for h in range(2):
            start(core_copy(p, 0, h))

    events = []
    for s in range(bits):
        for h in range(2):
            before = orders[h][:s]
            for m in range(chips):
                if m & ~sum(1 << b for b in before) == 0:
                    events.append((s, bin(m).count("1"), m | 1 << orders[h][s], h))
    events.sort()

    def arrive(p, event):
        s, _, r, h = event
        chip_arrival(p, r, h)
        for bit in orders[h][s + 1:]:
            start(chip_copy(p, r, h, bit))
        start(core_copy(p, r, h))

    tile = tile_of(unit, min(unit, 256), 512)

    def accumulate(p, first, count):
        for r in range(first, first + count):
            for h in range(2):
                core_arrival(p, r, h)
            if p == 0:
                load_work(r).wait()
        if first == 0:
            load_own(p).wait()

        def step(i, carry):
            r = lax.div(i, unit // tile) + first
            at = chip
            for b in range(bits):
                set_bit = lax.rem(lax.div(r, 1 << b), 2)
                have = lax.rem(lax.div(chip, 1 << b), 2)
                at = at + (1 << b) * set_bit * (1 - 2 * have)
            start_row = pl.multiple_of(at * unit + lax.rem(i, unit // tile) * tile, tile)
            inner[...] += left_product(vectors[p, pl.ds(start_row, tile)], work[pl.ds(start_row, tile)])
            return carry

        lax.fori_loop(0, count * (unit // tile), step, 0)

    def make_scaled(p):
        found = left_product(leaf_t[p], inner[...])
        high, low = halves(found)
        scaled[0] = high
        scaled[1] = low
        inner[...] = jnp.zeros_like(inner)

    down = tile_of(rows - width, width, 768)

    def store_rows(i):
        span = pl.ds(pl.multiple_of(width + i * down, width), down)
        return pltpu.make_async_copy(work.at[span], out.at[span], store_sem.at[1])

    def subtract(p, last):
        def step(i, carry):
            span = pl.ds(pl.multiple_of(width + i * down, width), down)
            work[span] = work[span] - right_product(vectors[p, span], (scaled[0], scaled[1]))
            return carry

        lax.fori_loop(0, (rows - width) // down, step, 0)

    def top_copy(p, level):
        return pltpu.make_async_remote_copy(
            top, other.at[p, level], top_send.at[p, level], top_recv.at[p, level],
            device_id={"row": flip(position, 1 << level), "col": column}, device_id_type=MESH)

    def active(level):
        return lax.rem(position, 1 << level) == 0

    def send_top(p, level):
        @pl.when(active(level))
        def _():
            top_copy(p, level).start()

    def combine(p, level):
        for copy in load_pair(p, level):
            copy.wait()

        @pl.when(active(level))
        def _():
            lower = lax.rem(lax.div(position, 1 << level), 2)
            own = pair_v[p, level, pl.ds(pl.multiple_of(lower * width, width), width)]
            theirs = pair_v[p, level, pl.ds(pl.multiple_of((1 - lower) * width, width), width)]
            inside = left_product(own, top[...])
            copy = top_copy(p, level)
            copy.wait_recv()
            inside = inside + left_product(theirs, other[p, level])
            weight = left_product(pair_t[p, level], inside)
            change = right_product(own, halves(weight))
            copy.wait_send()
            top[...] = top[...] - change

    inner[...] = jnp.zeros_like(inner)
    send_own(0)
    accumulate(0, 0, 1)
    early, late = events[:-2], events[-2:]
    for event in early:
        arrive(0, event)
    if panels > 1:
        send_own(1)
    accumulate(0, 1, chips - 2)
    for event in late:
        arrive(0, event)
    accumulate(0, chips - 1, 1)
    make_scaled(0)
    for p in range(panels):
        if p == 0:
            before_top = work[:width]
        else:
            before_top = top[...]
        top[...] = before_top - right_product(vectors[p, :width], (scaled[0], scaled[1]))
        send_top(p, 0)
        subtract(p, p == panels - 1)
        if p == panels - 1:
            span = pl.ds(width, rows - width)
            rest = pltpu.make_async_copy(work.at[span], out.at[span], store_sem.at[1])
            rest.start()
            for level in range(levels):
                combine(p, level)
                if level + 1 < levels:
                    send_top(p, level + 1)
            last = pltpu.make_async_copy(top, out.at[pl.ds(0, width)], store_sem.at[0])
            last.start()
            last.wait()
            rest.wait()
            break
        q = p + 1
        work[:width] = jnp.zeros((width, work.shape[1]), jnp.float32)
        first = len(events) - 4
        for event in events[:first]:
            arrive(q, event)
        accumulate(q, 0, 1)
        for event in events[first:-2]:
            arrive(q, event)
        if q + 1 < panels:
            send_own(q + 1)
        combine(p, 0)
        if levels > 1:
            send_top(p, 1)
        accumulate(q, 1, chips - 2)
        for event in late:
            arrive(q, event)
        accumulate(q, chips - 1, 1)
        for level in range(1, levels):
            combine(p, level)
            if level + 1 < levels:
                send_top(p, level + 1)
        inner[...] += left_product(vectors[q, :width], top[...])
        make_scaled(q)
    for copy in started:
        copy.wait_send()


def solution(mesh):
    grid_rows = mesh.shape["row"]
    chips = mesh.shape["col"] // 2
    levels = grid_rows.bit_length() - 1
    bits = chips.bit_length() - 1

    def local(matrix, leaf_v, leaf_t, tree_v, tree_t):
        rows, columns = matrix.shape
        panels, _, width = leaf_v.shape
        f32, dma = jnp.float32, pltpu.SemaphoreType.DMA
        hbm = pl.BlockSpec(memory_space=pl.ANY)
        vmem = pl.BlockSpec(memory_space=pltpu.VMEM)
        return pl.pallas_call(
            functools.partial(kernel, grid_rows, chips),
            out_shape=jax.ShapeDtypeStruct(matrix.shape, f32),
            in_specs=[hbm, hbm, vmem, hbm, hbm],
            out_specs=hbm,
            scratch_shapes=[
                pltpu.VMEM((rows, columns), f32),
                pltpu.VMEM((panels, rows, width), f32),
                pltpu.VMEM((width, columns), f32),
                pltpu.VMEM((2, width, columns), jnp.bfloat16),
                pltpu.VMEM((width, columns), f32),
                pltpu.VMEM((panels, levels, width, columns), f32),
                pltpu.VMEM((panels, levels, 2 * width, width), f32),
                pltpu.VMEM((panels, levels, width, width), f32),
                dma((panels + chips,)),
                dma((panels, levels, 2)),
                dma((2,)),
                dma((panels, chips, 2, bits)),
                dma((panels, chips, 2)),
                dma((panels, chips, 2)),
                dma((panels, chips, 2)),
                dma((panels, levels)),
                dma((panels, levels)),
            ],
            compiler_params=pltpu.CompilerParams(
                collective_id=0, has_side_effects=True, vmem_limit_bytes=56 * 1024 * 1024
            ),
        )(matrix, leaf_v, leaf_t, tree_v, tree_t)

    placed = (P("row", "col"), P(None, ("row", "col"), None), P(None, "row", None), P(), P())
    return jax.shard_map(local, mesh=mesh, in_specs=placed, out_specs=P("row", "col"), check_vma=False)
```

profile of v0, /device:TPU:0, one launch (start us, length us, event | category | flops | bytes accessed | tf_op | source)
XLA Modules:
  0.0 93.6 jit_solution(8177457335158612740)
XLA Ops:
  0.0 85.9 %shard_map.55 = f32[4096,512]{1,0:T(8,128)} custom-call(f32[4096,512]{1,0:T(8,128)} %matrix.1, f32[2,512,256]{2,1,0:T(8,128)} %leaf_v.1, f32[2,256,256]{2,1,0:T(8,128)} %leaf_t.1, f32[2,3,512,256]{3,2,1,0:T(8,128)} %tree_v.1, f32[2,3,256,256]{3,2,1,0:T(8,128)} %tree_t.1), custom_call_target="tpu_custom_call" | custom-call | tf_op jit(solution)/shard_map/pallas_call | solution.py:308
  85.9 7.8 %copy.7 = f32[4096,512]{1,0:T(8,128)} copy(f32[4096,512]{1,0:T(8,128)} %shard_map.55) | data formatting | bytes 16777216
where the time goes:
time: 93.8 us; the launch traced here: 93.6 us
  Pallas kernels  85.9 us (92%)
  local copies, waits for them, and re-layouts  7.76 us (8%)
    pallas_call x1, Pallas kernels, local(): pl.pallas_call(functools.partial(kernel, grid_rows, chips), out_shape=jax...  85.9 us
    unnamed x1, local copies, waits for them, and re-layouts  7.76 us

commit v1 on v0

--- a/solution.py
+++ b/solution.py
@@ -47,7 +47,7 @@
 
 
 def kernel(grid_rows, chips, matrix, leaf_v, leaf_t, tree_v, tree_t, out,
-           work, vectors, inner, scaled, top, other, pair_v, pair_t,
+           work, vectors, inner, scaled, top, hub, other, pair_v, pair_t,
            load_sem, tree_sem, store_sem, send_sem, recv_sem, core_send, core_recv, top_send, top_recv):
     panels, own_rows, width = leaf_v.shape
     rows = work.shape[0]
@@ -89,7 +89,9 @@
     barrier = pltpu.get_barrier_semaphore()
     partners = [device(chip, 1 - core)]
     partners += [device(flip(chip, 1 << b), core) for b in range(bits)]
-    partners += [{"row": flip(position, 1 << level), "col": column} for level in range(levels)]
+    sideways = {"row": flip(position, 1), "col": column}
+    across = {"row": grid_rows - 1 - position, "col": column}
+    partners += [sideways, across]
     for partner in partners:
         pl.semaphore_signal(barrier, inc=1, device_id=partner, device_id_type=MESH)
     pl.semaphore_wait(barrier, len(partners))
@@ -180,20 +182,9 @@
 
         lax.fori_loop(0, count * (unit // tile), step, 0)
 
-    def make_scaled(p):
-        found = left_product(leaf_t[p], inner[...])
-        high, low = halves(found)
-        scaled[0] = high
-        scaled[1] = low
-        inner[...] = jnp.zeros_like(inner)
-
     down = tile_of(rows - width, width, 768)
 
-    def store_rows(i):
-        span = pl.ds(pl.multiple_of(width + i * down, width), down)
-        return pltpu.make_async_copy(work.at[span], out.at[span], store_sem.at[1])
-
-    def subtract(p, last):
+    def subtract(p):
         def step(i, carry):
             span = pl.ds(pl.multiple_of(width + i * down, width), down)
             work[span] = work[span] - right_product(vectors[p, span], (scaled[0], scaled[1]))
@@ -201,42 +192,95 @@
 
         lax.fori_loop(0, (rows - width) // down, step, 0)
 
-    def top_copy(p, level):
+    chunks, _, part = top.shape
+    low, middle_low, middle_high = position == 0, position == 1, position == 2
+    middle = jnp.logical_or(middle_low, middle_high)
+
+    def exchange(buffer, p, j, stage, target):
         return pltpu.make_async_remote_copy(
-            top, other.at[p, level], top_send.at[p, level], top_recv.at[p, level],
-            device_id={"row": flip(position, 1 << level), "col": column}, device_id_type=MESH)
-
-    def active(level):
-        return lax.rem(position, 1 << level) == 0
-
-    def send_top(p, level):
-        @pl.when(active(level))
-        def _():
-            top_copy(p, level).start()
-
-    def combine(p, level):
-        for copy in load_pair(p, level):
-            copy.wait()
-
-        @pl.when(active(level))
-        def _():
-            lower = lax.rem(lax.div(position, 1 << level), 2)
-            own = pair_v[p, level, pl.ds(pl.multiple_of(lower * width, width), width)]
-            theirs = pair_v[p, level, pl.ds(pl.multiple_of((1 - lower) * width, width), width)]
-            inside = left_product(own, top[...])
-            copy = top_copy(p, level)
+            buffer, other.at[p, j, stage], top_send.at[p, j, stage], top_recv.at[p, j, stage],
+            device_id=target, device_id_type=MESH)
+
+    def head(p, j):
+        columns = slice(j * part, (j + 1) * part)
+        before = work[:width, columns] if p == 0 else top[j]
+        inside = inner[:, columns]
+        if p > 0:
+            inside = inside + left_product(vectors[p, :width], before)
+        weight = halves(left_product(leaf_t[p], inside))
+        scaled[0, :, columns], scaled[1, :, columns] = weight
+        top[j] = before - right_product(vectors[p, :width], weight)
+
+        @pl.when(jnp.logical_not(middle_low))
+        def _():
+            exchange(top.at[j], p, j, 0, sideways).start()
+
+    def first_level(p, j):
+        if j == 0:
+            for level in range(levels):
+                for copy in load_pair(p, level):
+                    copy.wait()
+
+        @pl.when(jnp.logical_not(low))
+        def _():
+            lower = lax.rem(position, 2)
+            own = pair_v[p, 0, pl.ds(pl.multiple_of(lower * width, width), width)]
+            theirs = pair_v[p, 0, pl.ds(pl.multiple_of((1 - lower) * width, width), width)]
+            inside = left_product(own, top[j])
+            exchange(top.at[j], p, j, 0, sideways).wait_recv()
+            inside = inside + left_product(theirs, other[p, j, 0])
+            weight = halves(left_product(pair_t[p, 0], inside))
+
+            @pl.when(middle_low)
+            def _():
+                hub[p, j] = other[p, j, 0] - right_product(theirs, weight)
+                exchange(hub.at[p, j], p, j, 1, across).start()
+                top[j] = top[j] - right_product(own, weight)
+
+            @pl.when(jnp.logical_not(middle_low))
+            def _():
+                change = right_product(own, weight)
+                exchange(top.at[j], p, j, 0, sideways).wait_send()
+                top[j] = top[j] - change
+
+            @pl.when(middle_high)
+            def _():
+                exchange(top.at[j], p, j, 1, across).start()
+
+    def second_level(p, j):
+        def update(buffer, half):
+            own = pair_v[p, 1, half * width:(half + 1) * width]
+            theirs = pair_v[p, 1, (1 - half) * width:(2 - half) * width]
+            inside = left_product(own, buffer[...])
+            copy = exchange(buffer, p, j, 1, across)
             copy.wait_recv()
-            inside = inside + left_product(theirs, other[p, level])
-            weight = left_product(pair_t[p, level], inside)
-            change = right_product(own, halves(weight))
+            inside = inside + left_product(theirs, other[p, j, 1])
+            weight = halves(left_product(pair_t[p, 1], inside))
+            change = right_product(own, weight)
             copy.wait_send()
-            top[...] = top[...] - change
-
+            buffer[...] = buffer[...] - change
+
+        @pl.when(middle_low)
+        def _():
+            update(hub.at[p, j], 0)
+            exchange(hub.at[p, j], p, j, 2, sideways).start()
+
+        @pl.when(middle_high)
+        def _():
+            update(top.at[j], 1)
+
+    def finish(p, j):
+        @pl.when(low)
+        def _():
+            exchange(top.at[j], p, j, 0, sideways).wait_send()
+            exchange(hub.at[p, j], p, j, 2, sideways).wait_recv()
+            top[j] = other[p, j, 2]
+
+    stage_one, stage_two, late = events[:-4], events[-4:-2], events[-2:]
     inner[...] = jnp.zeros_like(inner)
     send_own(0)
     accumulate(0, 0, 1)
-    early, late = events[:-2], events[-2:]
-    for event in early:
+    for event in stage_one + stage_two:
         arrive(0, event)
     if panels > 1:
         send_own(1)
@@ -244,51 +288,57 @@
     for event in late:
         arrive(0, event)
     accumulate(0, chips - 1, 1)
-    make_scaled(0)
+    for j in range(chunks):
+        head(0, j)
     for p in range(panels):
-        if p == 0:
-            before_top = work[:width]
-        else:
-            before_top = top[...]
-        top[...] = before_top - right_product(vectors[p, :width], (scaled[0], scaled[1]))
-        send_top(p, 0)
-        subtract(p, p == panels - 1)
-        if p == panels - 1:
+        q = p + 1
+        if q == panels:
+            first_level(p, 0)
+            first_level(p, 1)
+            for j in range(2, chunks):
+                first_level(p, j)
+            subtract(p)
             span = pl.ds(width, rows - width)
-            rest = pltpu.make_async_copy(work.at[span], out.at[span], store_sem.at[1])
+            rest = pltpu.make_async_copy(work.at[span], out.at[span], store_sem.at[chunks])
             rest.start()
-            for level in range(levels):
-                combine(p, level)
-                if level + 1 < levels:
-                    send_top(p, level + 1)
-            last = pltpu.make_async_copy(top, out.at[pl.ds(0, width)], store_sem.at[0])
-            last.start()
-            last.wait()
+            for j in range(chunks):
+                second_level(p, j)
+            last = []
+            for j in range(chunks):
+                finish(p, j)
+                copy = pltpu.make_async_copy(
+                    top.at[j], out.at[pl.ds(0, width), pl.ds(j * part, part)], store_sem.at[j])
+                copy.start()
+                last.append(copy)
+            for copy in last:
+                copy.wait()
             rest.wait()
             break
-        q = p + 1
+        subtract(p)
         work[:width] = jnp.zeros((width, work.shape[1]), jnp.float32)
-        first = len(events) - 4
-        for event in events[:first]:
-            arrive(q, event)
-        accumulate(q, 0, 1)
-        for event in events[first:-2]:
-            arrive(q, event)
+        inner[...] = jnp.zeros_like(inner)
+        todo = [functools.partial(arrive, q, event) for event in stage_one]
+        todo += [functools.partial(first_level, p, j) for j in range(2)]
+        todo += [functools.partial(accumulate, q, 0, 1)]
+        todo += [functools.partial(arrive, q, event) for event in stage_two]
         if q + 1 < panels:
-            send_own(q + 1)
-        combine(p, 0)
-        if levels > 1:
-            send_top(p, 1)
-        accumulate(q, 1, chips - 2)
-        for event in late:
-            arrive(q, event)
-        accumulate(q, chips - 1, 1)
-        for level in range(1, levels):
-            combine(p, level)
-            if level + 1 < levels:
-                send_top(p, level + 1)
-        inner[...] += left_product(vectors[q, :width], top[...])
-        make_scaled(q)
+            todo += [functools.partial(send_own, q + 1)]
+        todo += [functools.partial(first_level, p, 2), functools.partial(second_level, p, 0)]
+        todo += [functools.partial(accumulate, q, 1, chips - 2)]
+        todo += [functools.partial(first_level, p, 3), functools.partial(second_level, p, 1)]
+        todo += [functools.partial(arrive, q, event) for event in late]
+        todo += [functools.partial(second_level, p, 2), functools.partial(accumulate, q, chips - 1, 1)]
+        todo += [functools.partial(second_level, p, 3)]
+        for step in todo:
+            step()
+        for j in range(chunks):
+            finish(p, j)
+            head(q, j)
+    for p in range(panels):
+        for j in range(chunks):
+            @pl.when(middle_low)
+            def _(p=p, j=j):
+                exchange(hub.at[p, j], p, j, 2, sideways).wait_send()
     for copy in started:
         copy.wait_send()
 
@@ -301,6 +351,8 @@
 
     def local(matrix, leaf_v, leaf_t, tree_v, tree_t):
         rows, columns = matrix.shape
+        chunks = 4
+        part = columns // chunks
         panels, _, width = leaf_v.shape
         f32, dma = jnp.float32, pltpu.SemaphoreType.DMA
         hbm = pl.BlockSpec(memory_space=pl.ANY)
@@ -315,19 +367,20 @@
                 pltpu.VMEM((panels, rows, width), f32),
                 pltpu.VMEM((width, columns), f32),
                 pltpu.VMEM((2, width, columns), jnp.bfloat16),
-                pltpu.VMEM((width, columns), f32),
-                pltpu.VMEM((panels, levels, width, columns), f32),
+                pltpu.VMEM((chunks, width, part), f32),
+                pltpu.VMEM((panels, chunks, width, part), f32),
+                pltpu.VMEM((panels, chunks, 3, width, part), f32),
                 pltpu.VMEM((panels, levels, 2 * width, width), f32),
                 pltpu.VMEM((panels, levels, width, width), f32),
                 dma((panels + chips,)),
                 dma((panels, levels, 2)),
-                dma((2,)),
+                dma((chunks + 1,)),
                 dma((panels, chips, 2, bits)),
                 dma((panels, chips, 2)),
                 dma((panels, chips, 2)),
                 dma((panels, chips, 2)),
-                dma((panels, levels)),
-                dma((panels, levels)),
+                dma((panels, chunks, 3)),
+                dma((panels, chunks, 3)),
             ],
             compiler_params=pltpu.CompilerParams(
                 collective_id=0, has_side_effects=True, vmem_limit_bytes=56 * 1024 * 1024

time: 93.8 us -> 91.6 us (0.977)
  Pallas kernels: 85.9 us -> 83.7 us
    pallas_call x1, Pallas kernels: 85.9 us -> 83.7 us  [local(): pl.pallas_call(functools.partial(kernel, grid_rows, chips), out_shape=jax...]
where the time goes in v1:
time: 91.6 us; the launch traced here: 91.5 us
  Pallas kernels  83.7 us (91%)
  local copies, waits for them, and re-layouts  7.76 us (8%)
    pallas_call x1, Pallas kernels, local(): pl.pallas_call(functools.partial(kernel, grid_rows, chips), out_shape=jax...  83.7 us
    unnamed x1, local copies, waits for them, and re-layouts  7.76 us

profile of v1, /device:TPU:0, one launch (start us, length us, event | category | flops | bytes accessed | tf_op | source)
XLA Modules:
  0.0 91.5 jit_solution(12902529020487625913)
XLA Ops:
  0.0 83.7 %shard_map.55 = f32[4096,512]{1,0:T(8,128)} custom-call(f32[4096,512]{1,0:T(8,128)} %matrix.1, f32[2,512,256]{2,1,0:T(8,128)} %leaf_v.1, f32[2,256,256]{2,1,0:T(8,128)} %leaf_t.1, f32[2,3,512,256]{3,2,1,0:T(8,128)} %tree_v.1, f32[2,3,256,256]{3,2,1,0:T(8,128)} %tree_t.1), custom_call_target="tpu_custom_call" | custom-call | tf_op jit(solution)/shard_map/pallas_call | solution.py:360
  83.7 7.8 %copy.7 = f32[4096,512]{1,0:T(8,128)} copy(f32[4096,512]{1,0:T(8,128)} %shard_map.55) | data formatting | bytes 16777216

commit v2 on v1

--- a/solution.py
+++ b/solution.py
@@ -47,7 +47,7 @@
 
 
 def kernel(grid_rows, chips, matrix, leaf_v, leaf_t, tree_v, tree_t, out,
-           work, vectors, inner, scaled, top, hub, other, pair_v, pair_t,
+           work, vectors, inner, scaled, top, hub, other, pair_v, pair_t, node_map,
            load_sem, tree_sem, store_sem, send_sem, recv_sem, core_send, core_recv, top_send, top_recv):
     panels, own_rows, width = leaf_v.shape
     rows = work.shape[0]
@@ -184,13 +184,15 @@
 
     down = tile_of(rows - width, width, 768)
 
-    def subtract(p):
+    downs = (rows - width) // down
+
+    def subtract(p, first, last):
         def step(i, carry):
             span = pl.ds(pl.multiple_of(width + i * down, width), down)
             work[span] = work[span] - right_product(vectors[p, span], (scaled[0], scaled[1]))
             return carry
 
-        lax.fori_loop(0, (rows - width) // down, step, 0)
+        lax.fori_loop(first, last, step, 0)
 
     chunks, _, part = top.shape
     low, middle_low, middle_high = position == 0, position == 1, position == 2
@@ -201,47 +203,56 @@
             buffer, other.at[p, j, stage], top_send.at[p, j, stage], top_recv.at[p, j, stage],
             device_id=target, device_id_type=MESH)
 
-    def head(p, j):
-        columns = slice(j * part, (j + 1) * part)
-        before = work[:width, columns] if p == 0 else top[j]
-        inside = inner[:, columns]
+    def prepare(p):
+        for level in range(levels):
+            for copy in load_pair(p, level):
+                copy.wait()
+            pair = halves(pair_v[p, level])
+            weight = product(halves(pair_t[p, level]), pair, ((0,), (1,)))
+            whole = right_product(pair_v[p, level], halves(weight))
+            node_map[p, level, 0], node_map[p, level, 1] = halves(whole)
+
+    def mapped(p, level, to, count, source, value):
+        block = (pl.ds(to, count), pl.ds(source, width))
+        return product((node_map[(p, level, 0) + block], node_map[(p, level, 1) + block]), halves(value), ((1,), (0,)))
+
+    def head(p):
+        inside = inner[...]
         if p > 0:
-            inside = inside + left_product(vectors[p, :width], before)
+            inside = inside + left_product(vectors[p, :width], jnp.concatenate([top[j] for j in range(chunks)], axis=1))
         weight = halves(left_product(leaf_t[p], inside))
-        scaled[0, :, columns], scaled[1, :, columns] = weight
-        top[j] = before - right_product(vectors[p, :width], weight)
-
-        @pl.when(jnp.logical_not(middle_low))
+        scaled[0], scaled[1] = weight
+        above = halves(vectors[p, :width])
+        for j in range(chunks):
+            columns = slice(j * part, (j + 1) * part)
+            before = work[:width, columns] if p == 0 else top[j]
+            top[j] = before - product(above, (weight[0][:, columns], weight[1][:, columns]), ((1,), (0,)))
+
+            @pl.when(jnp.logical_not(middle_low))
+            def _(j=j):
+                exchange(top.at[j], p, j, 0, sideways).start()
+
+    def first_level(p, j):
+        @pl.when(middle_low)
         def _():
-            exchange(top.at[j], p, j, 0, sideways).start()
-
-    def first_level(p, j):
-        if j == 0:
-            for level in range(levels):
-                for copy in load_pair(p, level):
-                    copy.wait()
-
-        @pl.when(jnp.logical_not(low))
+            change = mapped(p, 0, 0, 2 * width, width, top[j])
+            exchange(top.at[j], p, j, 0, sideways).wait_recv()
+            theirs = other[p, j, 0]
+            change = change + mapped(p, 0, 0, 2 * width, 0, theirs)
+            hub[p, j] = theirs - change[:width]
+            exchange(hub.at[p, j], p, j, 1, across).start()
+            top[j] = top[j] - change[width:]
+
+        @pl.when(position > 1)
         def _():
-            lower = lax.rem(position, 2)
-            own = pair_v[p, 0, pl.ds(pl.multiple_of(lower * width, width), width)]
-            theirs = pair_v[p, 0, pl.ds(pl.multiple_of((1 - lower) * width, width), width)]
-            inside = left_product(own, top[j])
-            exchange(top.at[j], p, j, 0, sideways).wait_recv()
-            inside = inside + left_product(theirs, other[p, j, 0])
-            weight = halves(left_product(pair_t[p, 0], inside))
-
-            @pl.when(middle_low)
-            def _():
-                hub[p, j] = other[p, j, 0] - right_product(theirs, weight)
-                exchange(hub.at[p, j], p, j, 1, across).start()
-                top[j] = top[j] - right_product(own, weight)
-
-            @pl.when(jnp.logical_not(middle_low))
-            def _():
-                change = right_product(own, weight)
-                exchange(top.at[j], p, j, 0, sideways).wait_send()
-                top[j] = top[j] - change
+            mine = pl.multiple_of(lax.rem(position, 2) * width, width)
+            theirs = pl.multiple_of(width - lax.rem(position, 2) * width, width)
+            change = mapped(p, 0, mine, width, mine, top[j])
+            copy = exchange(top.at[j], p, j, 0, sideways)
+            copy.wait_recv()
+            change = change + mapped(p, 0, mine, width, theirs, other[p, j, 0])
+            copy.wait_send()
+            top[j] = top[j] - change
 
             @pl.when(middle_high)
             def _():
@@ -249,14 +260,11 @@
 
     def second_level(p, j):
         def update(buffer, half):
-            own = pair_v[p, 1, half * width:(half + 1) * width]
-            theirs = pair_v[p, 1, (1 - half) * width:(2 - half) * width]
-            inside = left_product(own, buffer[...])
+            mine, theirs = half * width, (1 - half) * width
+            change = mapped(p, 1, mine, width, mine, buffer[...])
             copy = exchange(buffer, p, j, 1, across)
             copy.wait_recv()
-            inside = inside + left_product(theirs, other[p, j, 1])
-            weight = halves(left_product(pair_t[p, 1], inside))
-            change = right_product(own, weight)
+            change = change + mapped(p, 1, mine, width, theirs, other[p, j, 1])
             copy.wait_send()
             buffer[...] = buffer[...] - change
 
@@ -280,6 +288,8 @@
     inner[...] = jnp.zeros_like(inner)
     send_own(0)
     accumulate(0, 0, 1)
+    for p in range(panels):
+        prepare(p)
     for event in stage_one + stage_two:
         arrive(0, event)
     if panels > 1:
@@ -288,20 +298,21 @@
     for event in late:
         arrive(0, event)
     accumulate(0, chips - 1, 1)
-    for j in range(chunks):
-        head(0, j)
+    head(0)
     for p in range(panels):
         q = p + 1
         if q == panels:
+            subtract(p, 0, downs // 2 + 1)
             first_level(p, 0)
             first_level(p, 1)
-            for j in range(2, chunks):
-                first_level(p, j)
-            subtract(p)
+            subtract(p, downs // 2 + 1, downs)
             span = pl.ds(width, rows - width)
             rest = pltpu.make_async_copy(work.at[span], out.at[span], store_sem.at[chunks])
             rest.start()
-            for j in range(chunks):
+            for j in range(2, chunks):
+                second_level(p, j - 2)
+                first_level(p, j)
+            for j in range(chunks - 2, chunks):
                 second_level(p, j)
             last = []
             for j in range(chunks):
@@ -314,7 +325,7 @@
                 copy.wait()
             rest.wait()
             break
-        subtract(p)
+        subtract(p, 0, downs)
         work[:width] = jnp.zeros((width, work.shape[1]), jnp.float32)
         inner[...] = jnp.zeros_like(inner)
         todo = [functools.partial(arrive, q, event) for event in stage_one]
@@ -333,7 +344,7 @@
             step()
         for j in range(chunks):
             finish(p, j)
-            head(q, j)
+        head(q)
     for p in range(panels):
         for j in range(chunks):
             @pl.when(middle_low)
@@ -372,6 +383,7 @@
                 pltpu.VMEM((panels, chunks, 3, width, part), f32),
                 pltpu.VMEM((panels, levels, 2 * width, width), f32),
                 pltpu.VMEM((panels, levels, width, width), f32),
+                pltpu.VMEM((panels, levels, 2, 2 * width, 2 * width), jnp.bfloat16),
                 dma((panels + chips,)),
                 dma((panels, levels, 2)),
                 dma((chunks + 1,)),

time: 91.6 us -> 90.3 us (0.986)
  Pallas kernels: 83.7 us -> 82.3 us
    pallas_call x1, Pallas kernels: 83.7 us -> 82.3 us  [local(): pl.pallas_call(functools.partial(kernel, grid_rows, chips), out_shape=jax...]
where the time goes in v2:
time: 90.3 us; the launch traced here: 90.1 us
  Pallas kernels  82.3 us (91%)
  local copies, waits for them, and re-layouts  7.76 us (9%)
    pallas_call x1, Pallas kernels, local(): pl.pallas_call(functools.partial(kernel, grid_rows, chips), out_shape=jax...  82.3 us
    unnamed x1, local copies, waits for them, and re-layouts  7.76 us

profile of v2, /device:TPU:0, one launch (start us, length us, event | category | flops | bytes accessed | tf_op | source)
XLA Modules:
  0.0 90.1 jit_solution(8862545363877025904)
XLA Ops:
  0.0 82.3 %shard_map.55 = f32[4096,512]{1,0:T(8,128)} custom-call(f32[4096,512]{1,0:T(8,128)} %matrix.1, f32[2,512,256]{2,1,0:T(8,128)} %leaf_v.1, f32[2,256,256]{2,1,0:T(8,128)} %leaf_t.1, f32[2,3,512,256]{3,2,1,0:T(8,128)} %tree_v.1, f32[2,3,256,256]{3,2,1,0:T(8,128)} %tree_t.1), custom_call_target="tpu_custom_call" | custom-call | tf_op jit(solution)/shard_map/pallas_call | solution.py:371
  82.3 7.8 %copy.7 = f32[4096,512]{1,0:T(8,128)} copy(f32[4096,512]{1,0:T(8,128)} %shard_map.55) | data formatting | bytes 16777216

commit v3 on v2

--- a/solution.py
+++ b/solution.py
@@ -217,20 +217,29 @@
         return product((node_map[(p, level, 0) + block], node_map[(p, level, 1) + block]), halves(value), ((1,), (0,)))
 
     def head(p):
-        inside = inner[...]
-        if p > 0:
-            inside = inside + left_product(vectors[p, :width], jnp.concatenate([top[j] for j in range(chunks)], axis=1))
-        weight = halves(left_product(leaf_t[p], inside))
+        weight = halves(left_product(leaf_t[p], inner[...]))
         scaled[0], scaled[1] = weight
         above = halves(vectors[p, :width])
         for j in range(chunks):
             columns = slice(j * part, (j + 1) * part)
-            before = work[:width, columns] if p == 0 else top[j]
+            before = work[:width, columns]
             top[j] = before - product(above, (weight[0][:, columns], weight[1][:, columns]), ((1,), (0,)))
 
             @pl.when(jnp.logical_not(middle_low))
             def _(j=j):
                 exchange(top.at[j], p, j, 0, sideways).start()
+
+    def head_part(p, j):
+        columns = slice(j * part, (j + 1) * part)
+        before = top[j]
+        inside = inner[:, columns] + left_product(vectors[p, :width], before)
+        weight = halves(left_product(leaf_t[p], inside))
+        scaled[0, :, columns], scaled[1, :, columns] = weight
+        top[j] = before - right_product(vectors[p, :width], weight)
+
+        @pl.when(jnp.logical_not(middle_low))
+        def _():
+            exchange(top.at[j], p, j, 0, sideways).start()
 
     def first_level(p, j):
         @pl.when(middle_low)
@@ -344,7 +353,7 @@
             step()
         for j in range(chunks):
             finish(p, j)
-        head(q)
+            head_part(q, j)
     for p in range(panels):
         for j in range(chunks):
             @pl.when(middle_low)
@@ -366,13 +375,13 @@
         part = columns // chunks
         panels, _, width = leaf_v.shape
         f32, dma = jnp.float32, pltpu.SemaphoreType.DMA
-        hbm = pl.BlockSpec(memory_space=pl.ANY)
+        hbm = pl.BlockSpec(memory_space=pltpu.HBM)
         vmem = pl.BlockSpec(memory_space=pltpu.VMEM)
         return pl.pallas_call(
             functools.partial(kernel, grid_rows, chips),
             out_shape=jax.ShapeDtypeStruct(matrix.shape, f32),
             in_specs=[hbm, hbm, vmem, hbm, hbm],
-            out_specs=hbm,
+            out_specs=pl.BlockSpec(memory_space=pl.ANY),
             scratch_shapes=[
                 pltpu.VMEM((rows, columns), f32),
                 pltpu.VMEM((panels, rows, width), f32),
@@ -395,7 +404,7 @@
                 dma((panels, chunks, 3)),
             ],
             compiler_params=pltpu.CompilerParams(
-                collective_id=0, has_side_effects=True, vmem_limit_bytes=56 * 1024 * 1024
+                collective_id=0, has_side_effects=True, vmem_limit_bytes=36 * 1024 * 1024
             ),
         )(matrix, leaf_v, leaf_t, tree_v, tree_t)
 

time: 90.3 us -> 84.3 us (0.934)
  Pallas kernels: 82.3 us -> 75.1 us
  local copies, waits for them, and re-layouts: 7.76 us -> 8.96 us
    pallas_call x1, Pallas kernels: 82.3 us -> 75.1 us  [local(): pl.pallas_call(functools.partial(kernel, grid_rows, chips), out_shape=jax...]
    unnamed x1 -> x9, local copies, waits for them, and re-layouts: 7.76 us -> 8.96 us
where the time goes in v3:
time: 84.3 us; the launch traced here: 84.1 us
  Pallas kernels  75.1 us (89%)
  local copies, waits for them, and re-layouts  8.96 us (11%)
    pallas_call x1, Pallas kernels, local(): pl.pallas_call(functools.partial(kernel, grid_rows, chips), out_shape=jax...  75.1 us
    unnamed x9, local copies, waits for them, and re-layouts  8.96 us

profile of v3, /device:TPU:0, one launch (start us, length us, event | category | flops | bytes accessed | tf_op | source)
XLA Modules:
  0.0 84.1 jit_solution(8487013127694836846)
XLA Ops:
  0.0 0.0 copy-start
  0.0 1.9 %copy-done = f32[2,3,512,256]{3,2,1,0:T(8,128)S(1)} copy-done((f32[2,3,512,256]{3,2,1,0:T(8,128)S(1)}, f32[2,3,512,256]{3,2,1,0:T(8,128)}, u32[]{:S(2)}) %copy-start) | copy-done | bytes 3145752
  1.9 0.0 copy-start.1
  1.9 1.4 %copy-done.1 = f32[2,3,256,256]{3,2,1,0:T(8,128)S(1)} copy-done((f32[2,3,256,256]{3,2,1,0:T(8,128)S(1)}, f32[2,3,256,256]{3,2,1,0:T(8,128)}, u32[]{:S(2)}) %copy-start.1) | copy-done | bytes 1572888
  3.3 0.0 copy-start.2
  3.3 1.2 %copy-done.2 = f32[2,512,256]{2,1,0:T(8,128)S(1)} copy-done((f32[2,512,256]{2,1,0:T(8,128)S(1)}, f32[2,512,256]{2,1,0:T(8,128)}, u32[]{:S(2)}) %copy-start.2) | copy-done | bytes 1048600
  4.5 0.0 copy-start.3
  4.5 1.0 %copy-done.3 = f32[2,256,256]{2,1,0:T(8,128)S(1)} copy-done((f32[2,256,256]{2,1,0:T(8,128)S(1)}, f32[2,256,256]{2,1,0:T(8,128)}, u32[]{:S(2)}) %copy-start.3) | copy-done | bytes 524312
  5.6 75.1 %shard_map.55 = f32[4096,512]{1,0:T(8,128)S(1)} custom-call(f32[4096,512]{1,0:T(8,128)} %matrix.1, f32[2,512,256]{2,1,0:T(8,128)S(1)} %copy-done.2, f32[2,256,256]{2,1,0:T(8,128)S(1)} %copy-done.3, f32[2,3,512,256]{3,2,1,0:T(8,128)S(1)} %copy-done, f32[2,3,256,256]{3,2,1,0:T(8,128)S(1)} %copy-done.1), custom_call_target="tpu_custom_call" | custom-call | tf_op jit(solution)/shard_map/pallas_call | solution.py:380
  80.7 3.4 %copy.7 = f32[4096,512]{1,0:T(8,128)} copy(f32[4096,512]{1,0:T(8,128)S(1)} %shard_map.55) | data formatting | bytes 16777216
Async XLA Ops:
  0.0 1.9 %copy-start = (f32[2,3,512,256]{3,2,1,0:T(8,128)S(1)}, f32[2,3,512,256]{3,2,1,0:T(8,128)}, u32[]{:S(2)}) copy-start(f32[2,3,512,256]{3,2,1,0:T(8,128)} %tree_v.1) | copy-start | bytes 9437188
  1.9 1.4 %copy-start.1 = (f32[2,3,256,256]{3,2,1,0:T(8,128)S(1)}, f32[2,3,256,256]{3,2,1,0:T(8,128)}, u32[]{:S(2)}) copy-start(f32[2,3,256,256]{3,2,1,0:T(8,128)} %tree_t.1) | copy-start | bytes 4718596
  3.3 1.2 %copy-start.2 = (f32[2,512,256]{2,1,0:T(8,128)S(1)}, f32[2,512,256]{2,1,0:T(8,128)}, u32[]{:S(2)}) copy-start(f32[2,512,256]{2,1,0:T(8,128)} %leaf_v.1) | copy-start | bytes 3145732
  4.5 1.0 %copy-start.3 = (f32[2,256,256]{2,1,0:T(8,128)S(1)}, f32[2,256,256]{2,1,0:T(8,128)}, u32[]{:S(2)}) copy-start(f32[2,256,256]{2,1,0:T(8,128)} %leaf_t.1) | copy-start | bytes 1572868
